TPU v7x, 32 devices: a whole 2x2x4 slice. The times are simulated.
32 devices in a mesh: ctx: 16 (over z, y, core), grp: 2 (over x).
Axes of the slice: x: 2, y: 2, z: 4, core: 2. Of those that a mesh axis runs over, the one named last changes fastest.
Arguments:
- query_in: bfloat16 [2560, 768], P(('grp', 'ctx')), parts along dimension 0, may hold values from -30 to 30
- key_in: bfloat16 [2560, 768], P(('grp', 'ctx')), parts along dimension 0, may hold values from -6 to 6
- value_in: bfloat16 [2560, 768], P(('grp', 'ctx')), parts along dimension 0, may hold values from -6 to 6
- length: int32 [2], P('grp'), parts along dimension 0, may hold values from 320 to 1280
- out_weight: bfloat16 [768, 1536], replicated, may hold values from -0.21875 to 0.21875
Outputs:
- projected: bfloat16 [2560, 1536], P(('grp', 'ctx')), parts along dimension 0
There are 2 independent parts, one for each index of `grp`. A program takes and returns all parts, laid end to end along the dimension named above; an argument that names none is the same for every part. Nothing has to cross between parts.
All inputs are finite; a program needn't handle non-finite values.
Results may differ from a plain program's by a relative error of at most 0.007.
Values may be sent and summed in bfloat16 or wider, within the bound.
A program may use at most 64 MiB of HBM per device.

v0:
```python
import jax
import jax.numpy as jnp
from jax import lax
from jax.sharding import PartitionSpec as P

HEADS = 12
HDIM = 64


def body(query_in, key_in, value_in, length, out_weight):
    local_rows = query_in.shape[0]
    offset = lax.axis_index("ctx") * local_rows
    valid_len = length[0]
    score_scale = 1.0 / jnp.sqrt(jnp.float32(HDIM))
    query_heads = query_in.reshape(local_rows, HEADS, HDIM).transpose(1, 0, 2)
    start_state = (
        jnp.full((HEADS, local_rows), -1e30, jnp.float32),
        jnp.zeros((HEADS, local_rows), jnp.float32),
        jnp.zeros((HEADS, local_rows, HDIM), jnp.float32),
    )
    key_part = lax.all_gather(key_in, "ctx", axis=0, tiled=True)
    value_part = lax.all_gather(value_in, "ctx", axis=0, tiled=True)
    part_rows = key_part.shape[0]
    key_live = (jnp.arange(part_rows, dtype=jnp.int32) < valid_len)[None, :]
    key_heads = key_part.reshape(part_rows, HEADS, HDIM).transpose(1, 0, 2)
    value_heads = value_part.reshape(part_rows, HEADS, HDIM).transpose(1, 0, 2)

    def fold_head(operands):
        query_h, key_h, value_h, run_max, run_sum, run_acc = operands
        scores = jnp.dot(query_h, key_h.T, preferred_element_type=jnp.float32) * score_scale
        new_max = jnp.maximum(
            run_max, jnp.max(jnp.where(key_live, scores, jnp.float32(-1e30)), axis=1)
        )
        expons = jnp.where(key_live, jnp.exp(scores - new_max[:, None]), jnp.float32(0.0))
        factor = jnp.exp(run_max - new_max)
        added = jnp.dot(expons.astype(jnp.bfloat16), value_h, preferred_element_type=jnp.float32)
        return (
            new_max,
            run_sum * factor + jnp.sum(expons, axis=1),
            run_acc * factor[:, None] + added,
        )

    running, denominator, weighted = lax.map(
        fold_head, (query_heads, key_heads, value_heads) + tuple(start_state)
    )
    heads_out = (
        (weighted / denominator[:, :, None]).transpose(1, 0, 2).reshape(local_rows, HEADS * HDIM)
    )
    query_live = offset + jnp.arange(local_rows, dtype=jnp.int32) < valid_len
    attended = jnp.where(query_live[:, None], heads_out, jnp.float32(0.0)).astype(jnp.bfloat16)
    return jnp.dot(attended, out_weight, preferred_element_type=jnp.float32).astype(jnp.bfloat16)


def solution(mesh):
    in_specs = (
        P(("grp", "ctx"), None),
        P(("grp", "ctx"), None),
        P(("grp", "ctx"), None),
        P("grp"),
        P(),
    )
    out_specs = P(("grp", "ctx"), None)
    return jax.shard_map(body, mesh=mesh, in_specs=in_specs, out_specs=out_specs, check_vma=False)
```

profile of v0, /device:TPU:0, one launch (start us, length us, event | category | flops | bytes accessed | tf_op | source)
XLA Modules:
  0.0 149.1 jit_solution(4521468957374590369)
XLA Ops:
  9.8 43.4 %all-gather.3.cloned.1.call-done = bf16[1280,768]{1,0:T(8,128)(2,1)} async-done(((bf16[80,768]{1,0:T(8,128)(2,1)}), bf16[1280,768]{1,0:T(8,128)(2,1)}) %all-gather.3.cloned.1.call-update) | async-done | bytes 1966096 | tf_op jit(solution)/shard_map/all_gather | solution.py:21
  53.2 4.0 %copy.13 = bf16[1280,768]{0,1:T(8,128)(2,1)} copy(bf16[1280,768]{1,0:T(8,128)(2,1)} %all-gather.3.cloned.1.call-done) | data formatting | bytes 3932160 | tf_op jit(solution)/shard_map/all_gather | solution.py:21
  57.2 38.1 %all-gather.5.cloned.1.call-done = bf16[1280,768]{1,0:T(8,128)(2,1)} async-done(((bf16[80,768]{1,0:T(8,128)(2,1)}), bf16[1280,768]{1,0:T(8,128)(2,1)}) %all-gather.5.cloned.1.call-update) | async-done | bytes 1966096 | tf_op jit(solution)/shard_map/all_gather | solution.py:22
  95.3 4.0 %copy.14 = bf16[1280,768]{0,1:T(8,128)(2,1)} copy(bf16[1280,768]{1,0:T(8,128)(2,1)} %all-gather.5.cloned.1.call-done) | data formatting | bytes 3932160 | tf_op jit(solution)/shard_map/all_gather | solution.py:22
  99.3 41.6 %while.13 = (s32[]{:T(128)}, f32[12,80]{1,0:T(8,128)S(1)}, f32[12,80,64]{1,2,0:T(8,128)S(1)}, bf16[12,80,64]{1,2,0:T(8,128)(2,1)S(1)}, bf16[12,1280,64]{1,2,0:T(...) while((s32[]{:T(128)}, f32[12,80]{1,0:T(8,128)S(1)}, ...), condition=%wide.region_3.4_spmd.clone, body=%wide.region_0.3_spmd.clone.sunk | while | flops 27142640 | bytes 1618981 | solution.py:43
  100.0 1.3 select_reduce_fusion.2
  101.5 1.2 fusion.29
  103.4 1.3 select_reduce_fusion.2
  106.9 1.3 select_reduce_fusion.2
  108.4 1.2 fusion.29
  110.4 1.3 select_reduce_fusion.2
  111.9 1.2 fusion.29
  113.8 1.3 select_reduce_fusion.2
  117.3 1.3 select_reduce_fusion.2
  118.8 1.2 fusion.29
  120.8 1.3 select_reduce_fusion.2
  122.3 1.2 fusion.29
  124.2 1.3 select_reduce_fusion.2
  127.7 1.3 select_reduce_fusion.2
  129.2 1.2 fusion.29
  131.2 1.3 select_reduce_fusion.2
  134.7 1.3 select_reduce_fusion.2
  138.1 1.3 select_reduce_fusion.2
  141.0 1.3 convolution_convert_fusion
  (78 shorter events, 21.5 us)
Async XLA Ops:
  6.5 134.5 %copy-start = (bf16[768,1536]{1,0:T(8,128)(2,1)S(1)}, bf16[768,1536]{1,0:T(8,128)(2,1)}, u32[]{:S(2)}) copy-start(bf16[768,1536]{1,0:T(8,128)(2,1)} %param.11) | copy-start | bytes 7077892
  6.5 46.7 %all-gather.3.cloned.1.call-start = ((), (), s32[]{:S(2)}) async-start(), calls=%async_computation | async-start | bytes 2088960 | tf_op jit(solution)/shard_map/all_gather | solution.py:21
  7.3 88.0 %all-gather.5.cloned.1.call-start = ((), (), s32[]{:S(2)}) async-start(), calls=%async_computation.1 | async-start | bytes 2088960 | tf_op jit(solution)/shard_map/all_gather | solution.py:22
Sparse Core Ops, SparseCore 0:
  9.6 43.5 all-gather.2
  55.5 39.7 all-gather.4
where the time goes:
time: 150 us; the launch traced here: 149 us
  waiting for transfers between devices  82.9 us (55%)
  matrix products  30.9 us (21%)
  between operations  14.1 us (9%)
  other arithmetic  11.3 us (8%)
  local copies, waits for them, and re-layouts  9.49 us (6%)
    all_gather x1, waiting for transfers between devices, body(): key_part = lax.all_gather(key_in, 'ctx', axis=0, tiled=True)  43.4 us
    all_gather x1, waiting for transfers between devices, body(): value_part = lax.all_gather(value_in, 'ctx', axis=0, tiled=True)  38.1 us
    dot_general x12, matrix products, fold_head(): jnp.dot(query_h, key_h.T, preferred_element_type=jnp.float32) * score_scale  15.2 us
    dot_general x12, matrix products, fold_head(): jnp.dot(expons.astype(jnp.bfloat16), value_h, preferred_element_type=jnp....  14.4 us
    lt x12, other arithmetic, body(): key_live = (jnp.arange(part_rows, dtype=jnp.int32) < valid_len)[None, :]  8.16 us
    all_gather x1, local copies, waits for them, and re-layouts, body(): value_part = lax.all_gather(value_in, 'ctx', axis=0, tiled=True)  4 us
    all_gather x1, local copies, waits for them, and re-layouts, body(): key_part = lax.all_gather(key_in, 'ctx', axis=0, tiled=True)  3.97 us
  transfers between devices with their start and end apart: 2, of which 2 were waited for; matrix products, arithmetic and copies ran while one was open for 3% of the time, Pallas kernels for 0%

commit v1 on v0

--- a/solution.py
+++ b/solution.py
@@ -18,8 +18,9 @@
         jnp.zeros((HEADS, local_rows), jnp.float32),
         jnp.zeros((HEADS, local_rows, HDIM), jnp.float32),
     )
-    key_part = lax.all_gather(key_in, "ctx", axis=0, tiled=True)
-    value_part = lax.all_gather(value_in, "ctx", axis=0, tiled=True)
+    view_out = jnp.concatenate([key_in, value_in], axis=1)
+    low = jax.lax.all_gather(view_out, "ctx", axis=0, tiled=True)
+    key_part, value_part = jnp.split(low, [key_in.shape[1]], axis=1)
     part_rows = key_part.shape[0]
     key_live = (jnp.arange(part_rows, dtype=jnp.int32) < valid_len)[None, :]
     key_heads = key_part.reshape(part_rows, HEADS, HDIM).transpose(1, 0, 2)

time: 150 us -> 124 us (0.83)
  waiting for transfers between devices: 82.9 us -> 51 us
  local copies, waits for them, and re-layouts: 9.49 us -> 13.8 us
  other arithmetic: 11.3 us -> 13.1 us
    all_gather x2 -> x1, waiting for transfers between devices: 81.5 us -> 51 us  [body(): low = jax.lax.all_gather(view_out, 'ctx', axis=0, tiled=True)]
    unnamed x3 -> x5, local copies, waits for them, and re-layouts: 1.07 us -> 9.04 us
    all_gather x2 -> x0, local copies, waits for them, and re-layouts: 7.96 us -> none  [the longest x1 4 us: body(): value_part = lax.all_gather(value_in, 'ctx', axis=0, tiled=True)]
    split x0 -> x1, local copies, waits for them, and re-layouts: none -> 4.29 us  [body(): key_part, value_part = jnp.split(low, [key_in.shape[1]], axis=1)]
    concatenate x0 -> x1, other arithmetic: none -> 1.82 us  [body(): view_out = jnp.concatenate([key_in, value_in], axis=1)]
  transfers between devices with their start and end apart: 2 -> 1, of which waited for: 2 -> 1; matrix products, arithmetic and copies ran while one was open for 3% -> 1% of each run, Pallas kernels for 0% -> 0%
where the time goes in v1:
time: 124 us; the launch traced here: 123 us
  waiting for transfers between devices  51 us (41%)
  matrix products  30.9 us (25%)
  between operations  14.1 us (11%)
  local copies, waits for them, and re-layouts  13.8 us (11%)
  other arithmetic  13.1 us (11%)
    all_gather x1, waiting for transfers between devices, body(): low = jax.lax.all_gather(view_out, 'ctx', axis=0, tiled=True)  51 us
    dot_general x12, matrix products, fold_head(): jnp.dot(query_h, key_h.T, preferred_element_type=jnp.float32) * score_scale  15.2 us
    dot_general x12, matrix products, fold_head(): jnp.dot(expons.astype(jnp.bfloat16), value_h, preferred_element_type=jnp....  14.4 us
    unnamed x5, local copies, waits for them, and re-layouts  9.04 us
    lt x12, other arithmetic, body(): key_live = (jnp.arange(part_rows, dtype=jnp.int32) < valid_len)[None, :]  8.16 us
    split x1, local copies, waits for them, and re-layouts, body(): key_part, value_part = jnp.split(low, [key_in.shape[1]], axis=1)  4.29 us
    reduce_sum x12, other arithmetic, fold_head(): jnp.sum(expons, axis=1)  2.83 us
  transfers between devices with their start and end apart: 1, of which 1 were waited for; matrix products, arithmetic and copies ran while one was open for 1% of the time, Pallas kernels for 0%

profile of v1, /device:TPU:0, one launch (start us, length us, event | category | flops | bytes accessed | tf_op | source)
XLA Modules:
  0.0 123.3 jit_solution(4527870961797993651)
XLA Ops:
  6.5 1.8 %pad_maximum_fusion = bf16[80,1536]{1,0:T(8,128)(2,1)} fusion(bf16[80,768]{1,0:T(8,128)(2,1)} %param.9, bf16[80,768]{1,0:T(8,128)(2,1)} %param.8), kind=kLoop, calls=%fused_computation.28 | loop fusion | flops 491520 | bytes 491520 | tf_op jit(solution)/shard_map/concatenate | solution.py:21
  10.1 51.0 %all-gather.2.cloned.1.call-done = bf16[1280,1536]{1,0:T(8,128)(2,1)} async-done(((bf16[80,1536]{1,0:T(8,128)(2,1)}), bf16[1280,1536]{1,0:T(8,128)(2,1)}) %all-gather.2.cloned.1.call-update) | async-done | bytes 3932176 | tf_op jit(solution)/shard_map/all_gather | solution.py:22
  61.2 4.3 %fusion.20 = (bf16[1280,768]{1,0:T(8,128)(2,1)}, bf16[1280,768]{1,0:T(8,128)(2,1)}) fusion(bf16[1280,1536]{1,0:T(8,128)(2,1)} %all-gather.2.cloned.1.call-done), kind=kLoop, calls=%fused_computation.31 | loop fusion | bytes 7864320 | tf_op jit(solution)/shard_map/split | solution.py:23
  65.5 4.0 %copy.21 = bf16[1280,768]{0,1:T(8,128)(2,1)} copy(bf16[1280,768]{1,0:T(8,128)(2,1)} %get-tuple-element.95) | data formatting | bytes 3932160
  69.5 4.0 %copy.22 = bf16[1280,768]{0,1:T(8,128)(2,1)} copy(bf16[1280,768]{1,0:T(8,128)(2,1)} %get-tuple-element.94) | data formatting | bytes 3932160
  73.4 41.6 %while.13 = (s32[]{:T(128)}, f32[12,80]{1,0:T(8,128)S(1)}, f32[12,80,64]{1,2,0:T(8,128)S(1)}, bf16[12,80,64]{1,2,0:T(8,128)(2,1)S(1)}, bf16[12,1280,64]{1,2,0:T(...) while((s32[]{:T(128)}, f32[12,80]{1,0:T(8,128)S(1)}, ...), condition=%wide.region_3.4_spmd.clone, body=%wide.region_0.3_spmd.clone.sunk | while | flops 27142640 | bytes 1618981 | solution.py:44
  74.1 1.3 %select_reduce_fusion.2 = (f32[80]{0:T(128)S(1)}, f32[80,1280]{1,0:T(8,128)S(1)}) fusion(pred[1280]{0:T(1024)(128)(4,1)S(1)} %compare_reduce_fusion.2, bf16[12,1280,64]{1,2,0:T(8,128)(2,1)} %get-tuple-element.169, s32[]{:T(128)} %get-tuple-element.156, bf16[12,80,64]{1,2,0:T(8,128)(2,1)S(1)} %get-tuple-element.168), kind=kOutput, calls=%fused_computation.6.clone.1 | convolution fusion | flops 13414320 | bytes 593216 | tf_op jit(solution)/shard_map/while/body/eval_jaxpr/dot_general | solution.py:31
  75.6 1.2 fusion.30
  77.6 1.3 %select_reduce_fusion.2 = (f32[80]{0:T(128)S(1)}, f32[80,1280]{1,0:T(8,128)S(1)}) fusion(pred[1280]{0:T(1024)(128)(4,1)S(1)} %compare_reduce_fusion.2, bf16[12,1280,64]{1,2,0:T(8,128)(2,1)} %get-tuple-element.169, s32[]{:T(128)} %get-tuple-element.156, bf16[12,80,64]{1,2,0:T(8,128)(2,1)S(1)} %get-tuple-element.168), kind=kOutput, calls=%fused_computation.6.clone.1 | convolution fusion | flops 13414320 | bytes 593216 | tf_op jit(solution)/shard_map/while/body/eval_jaxpr/dot_general | solution.py:31
  79.1 1.2 fusion.30
  81.0 1.3 %select_reduce_fusion.2 = (f32[80]{0:T(128)S(1)}, f32[80,1280]{1,0:T(8,128)S(1)}) fusion(pred[1280]{0:T(1024)(128)(4,1)S(1)} %compare_reduce_fusion.2, bf16[12,1280,64]{1,2,0:T(8,128)(2,1)} %get-tuple-element.169, s32[]{:T(128)} %get-tuple-element.156, bf16[12,80,64]{1,2,0:T(8,128)(2,1)S(1)} %get-tuple-element.168), kind=kOutput, calls=%fused_computation.6.clone.1 | convolution fusion | flops 13414320 | bytes 593216 | tf_op jit(solution)/shard_map/while/body/eval_jaxpr/dot_general | solution.py:31
  84.5 1.3 %select_reduce_fusion.2 = (f32[80]{0:T(128)S(1)}, f32[80,1280]{1,0:T(8,128)S(1)}) fusion(pred[1280]{0:T(1024)(128)(4,1)S(1)} %compare_reduce_fusion.2, bf16[12,1280,64]{1,2,0:T(8,128)(2,1)} %get-tuple-element.169, s32[]{:T(128)} %get-tuple-element.156, bf16[12,80,64]{1,2,0:T(8,128)(2,1)S(1)} %get-tuple-element.168), kind=kOutput, calls=%fused_computation.6.clone.1 | convolution fusion | flops 13414320 | bytes 593216 | tf_op jit(solution)/shard_map/while/body/eval_jaxpr/dot_general | solution.py:31
  86.0 1.2 fusion.30
  88.0 1.3 %select_reduce_fusion.2 = (f32[80]{0:T(128)S(1)}, f32[80,1280]{1,0:T(8,128)S(1)}) fusion(pred[1280]{0:T(1024)(128)(4,1)S(1)} %compare_reduce_fusion.2, bf16[12,1280,64]{1,2,0:T(8,128)(2,1)} %get-tuple-element.169, s32[]{:T(128)} %get-tuple-element.156, bf16[12,80,64]{1,2,0:T(8,128)(2,1)S(1)} %get-tuple-element.168), kind=kOutput, calls=%fused_computation.6.clone.1 | convolution fusion | flops 13414320 | bytes 593216 | tf_op jit(solution)/shard_map/while/body/eval_jaxpr/dot_general | solution.py:31
  89.5 1.2 fusion.30
  91.5 1.3 %select_reduce_fusion.2 = (f32[80]{0:T(128)S(1)}, f32[80,1280]{1,0:T(8,128)S(1)}) fusion(pred[1280]{0:T(1024)(128)(4,1)S(1)} %compare_reduce_fusion.2, bf16[12,1280,64]{1,2,0:T(8,128)(2,1)} %get-tuple-element.169, s32[]{:T(128)} %get-tuple-element.156, bf16[12,80,64]{1,2,0:T(8,128)(2,1)S(1)} %get-tuple-element.168), kind=kOutput, calls=%fused_computation.6.clone.1 | convolution fusion | flops 13414320 | bytes 593216 | tf_op jit(solution)/shard_map/while/body/eval_jaxpr/dot_general | solution.py:31
  94.9 1.3 %select_reduce_fusion.2 = (f32[80]{0:T(128)S(1)}, f32[80,1280]{1,0:T(8,128)S(1)}) fusion(pred[1280]{0:T(1024)(128)(4,1)S(1)} %compare_reduce_fusion.2, bf16[12,1280,64]{1,2,0:T(8,128)(2,1)} %get-tuple-element.169, s32[]{:T(128)} %get-tuple-element.156, bf16[12,80,64]{1,2,0:T(8,128)(2,1)S(1)} %get-tuple-element.168), kind=kOutput, calls=%fused_computation.6.clone.1 | convolution fusion | flops 13414320 | bytes 593216 | tf_op jit(solution)/shard_map/while/body/eval_jaxpr/dot_general | solution.py:31
  96.5 1.2 fusion.30
  98.4 1.3 %select_reduce_fusion.2 = (f32[80]{0:T(128)S(1)}, f32[80,1280]{1,0:T(8,128)S(1)}) fusion(pred[1280]{0:T(1024)(128)(4,1)S(1)} %compare_reduce_fusion.2, bf16[12,1280,64]{1,2,0:T(8,128)(2,1)} %get-tuple-element.169, s32[]{:T(128)} %get-tuple-element.156, bf16[12,80,64]{1,2,0:T(8,128)(2,1)S(1)} %get-tuple-element.168), kind=kOutput, calls=%fused_computation.6.clone.1 | convolution fusion | flops 13414320 | bytes 593216 | tf_op jit(solution)/shard_map/while/body/eval_jaxpr/dot_general | solution.py:31
  101.9 1.3 %select_reduce_fusion.2 = (f32[80]{0:T(128)S(1)}, f32[80,1280]{1,0:T(8,128)S(1)}) fusion(pred[1280]{0:T(1024)(128)(4,1)S(1)} %compare_reduce_fusion.2, bf16[12,1280,64]{1,2,0:T(8,128)(2,1)} %get-tuple-element.169, s32[]{:T(128)} %get-tuple-element.156, bf16[12,80,64]{1,2,0:T(8,128)(2,1)S(1)} %get-tuple-element.168), kind=kOutput, calls=%fused_computation.6.clone.1 | convolution fusion | flops 13414320 | bytes 593216 | tf_op jit(solution)/shard_map/while/body/eval_jaxpr/dot_general | solution.py:31
  105.3 1.3 %select_reduce_fusion.2 = (f32[80]{0:T(128)S(1)}, f32[80,1280]{1,0:T(8,128)S(1)}) fusion(pred[1280]{0:T(1024)(128)(4,1)S(1)} %compare_reduce_fusion.2, bf16[12,1280,64]{1,2,0:T(8,128)(2,1)} %get-tuple-element.169, s32[]{:T(128)} %get-tuple-element.156, bf16[12,80,64]{1,2,0:T(8,128)(2,1)S(1)} %get-tuple-element.168), kind=kOutput, calls=%fused_computation.6.clone.1 | convolution fusion | flops 13414320 | bytes 593216 | tf_op jit(solution)/shard_map/while/body/eval_jaxpr/dot_general | solution.py:31
  108.8 1.3 %select_reduce_fusion.2 = (f32[80]{0:T(128)S(1)}, f32[80,1280]{1,0:T(8,128)S(1)}) fusion(pred[1280]{0:T(1024)(128)(4,1)S(1)} %compare_reduce_fusion.2, bf16[12,1280,64]{1,2,0:T(8,128)(2,1)} %get-tuple-element.169, s32[]{:T(128)} %get-tuple-element.156, bf16[12,80,64]{1,2,0:T(8,128)(2,1)S(1)} %get-tuple-element.168), kind=kOutput, calls=%fused_computation.6.clone.1 | convolution fusion | flops 13414320 | bytes 593216 | tf_op jit(solution)/shard_map/while/body/eval_jaxpr/dot_general | solution.py:31
  112.3 1.3 %select_reduce_fusion.2 = (f32[80]{0:T(128)S(1)}, f32[80,1280]{1,0:T(8,128)S(1)}) fusion(pred[1280]{0:T(1024)(128)(4,1)S(1)} %compare_reduce_fusion.2, bf16[12,1280,64]{1,2,0:T(8,128)(2,1)} %get-tuple-element.169, s32[]{:T(128)} %get-tuple-element.156, bf16[12,80,64]{1,2,0:T(8,128)(2,1)S(1)} %get-tuple-element.168), kind=kOutput, calls=%fused_computation.6.clone.1 | convolution fusion | flops 13414320 | bytes 593216 | tf_op jit(solution)/shard_map/while/body/eval_jaxpr/dot_general | solution.py:31
  115.2 1.3 %convolution_convert_fusion = bf16[80,1536]{1,0:T(8,128)(2,1)} fusion(bf16[80,768]{0,1:T(8,128)(2,1)S(1)} %fusion.19, bf16[768,1536]{1,0:T(8,128)(2,1)S(1)} %copy-done), kind=kOutput, calls=%fused_computation.25 | convolution fusion | flops 188866560 | bytes 2727936 | tf_op jit(solution)/shard_map/dot_general | solution.py:52
  (77 shorter events, 21.2 us)
Async XLA Ops:
  6.5 108.6 %copy-start = (bf16[768,1536]{1,0:T(8,128)(2,1)S(1)}, bf16[768,1536]{1,0:T(8,128)(2,1)}, u32[]{:S(2)}) copy-start(bf16[768,1536]{1,0:T(8,128)(2,1)} %param.11) | copy-start | bytes 7077892
  6.5 54.6 %all-gather.2.cloned.1.call-start = ((), (), s32[]{:S(2)}) async-start(), calls=%async_computation | async-start | bytes 4177920 | tf_op jit(solution)/shard_map/all_gather | solution.py:22
Sparse Core Ops, SparseCore 0:
  9.6 51.4 all-gather.1
